TPU v7x, 32 devices: a whole 2x2x4 slice. The times are simulated.
32 devices in a mesh: grp: 4 (over y, x), dev: 8 (over z, core).
Axes of the slice: x: 2, y: 2, z: 4, core: 2. Of those that a mesh axis runs over, the one named last changes fastest.
Arguments:
- face_owner: int32 [131072, 1], P(('grp', 'dev')), may hold values from 0 to 31; in each aligned block of 4096 rows (0 to 4095, 4096 to 8191, ...) at most 256 rows name the same one
- face_element: int32 [131072], P(('grp', 'dev')), may hold values from 0 to 16383
- element_state: bfloat16 [110, 131072], P(None, ('grp', 'dev')), may hold values from -6 to 6
- lift: bfloat16 [30, 110], replicated, may hold values from -0.5 to 0.5
- face_scale: float32 [131072], P(('grp', 'dev')), may hold values from 0.5 to 2
- transfer: float32 [4, 10], replicated, may hold values from 0.05 to 0.5
- stiffness_ref: float32 [12, 12], replicated, may hold values from -0.18 to 5, as said below
- element_scale: float32 [256, 2048], P('grp', 'dev'), may hold values from 1 to 1.1
- displacement_prev: float32 [4, 3, 256, 2048], P(None, None, 'grp', 'dev'), may hold values from -6 to 6
Outputs:
- shell_displacement: float32 [4, 3, 256, 2048], P(None, None, 'grp', 'dev')
- face_displacement: float32 [3, 10, 131072], P(None, None, ('grp', 'dev'))
Inputs may be any that keep to these rules, and one draw needn't show every extreme that they name: `face_owner`: among the 4096 faces of one device (aligned blocks), at most 256 name the same owner, and in every draw some device has exactly 256 faces on one owner. `stiffness_ref`: every diagonal entry is 5 and the off-diagonal entries of each row have absolute values summing to at most 2.
All inputs are finite; a program needn't handle non-finite values.
Results may differ from a plain program's by a relative error of at most 0.0003.
Values sent between devices are 32-bit elements; how exact they have to be, the bound alone decides.
A program may use at most 128 MiB of HBM per device.

v0:
```python
import jax
import jax.numpy as jnp
from jax import lax
from jax.sharding import PartitionSpec as P

NODES_F = 10
SWEEPS = 8


coupling_weight = 2.2
highest = lax.Precision.HIGHEST


def with_halo(block, sides, width):
    for axis, dim in sides:
        count = lax.axis_size(axis)
        forward = [(i, i + 1) for i in range(count - 1)]
        backward = [(target, source) for source, target in forward]
        low = lax.ppermute(
            lax.slice_in_dim(block, block.shape[dim] - width, None, axis=dim), axis, forward
        )
        high = lax.ppermute(lax.slice_in_dim(block, 0, width, axis=dim), axis, backward)
        block = jnp.concatenate([low, block, high], axis=dim)
    return block


def invert_block(stiffness_ref):
    identity = jnp.eye(12, dtype=jnp.float32)
    approx = identity / 5.0
    for turn_index in range(8):
        product = jnp.dot(
            stiffness_ref, approx, precision=highest, preferred_element_type=jnp.float32
        )
        approx = jnp.dot(
            approx, 2.0 * identity - product, precision=highest, preferred_element_type=jnp.float32
        )
    return approx


def relax(padded, shell_load, block_inverse, scale):
    east_side = padded[:, :, 1:-1, 2:]
    west_side = padded[:, :, 1:-1, :-2]
    north_side = padded[:, :, 2:, 1:-1]
    south_side = padded[:, :, :-2, 1:-1]
    sources = [
        shell_load[0] + coupling_weight * (west_side[1] + south_side[2]),
        shell_load[1] + coupling_weight * (east_side[0] + south_side[3]),
        shell_load[2] + coupling_weight * (west_side[3] + north_side[0]),
        shell_load[3] + coupling_weight * (east_side[2] + north_side[1]),
    ]
    outputs = []
    for row_index in range(12):
        total = block_inverse[row_index, 0] * sources[0][0]
        for col_index in range(1, 12):
            total = (
                total + block_inverse[row_index, col_index] * sources[col_index // 3][col_index % 3]
            )
        outputs.append(total / scale)
    return jnp.stack(outputs).reshape(
        padded.shape[0], padded.shape[1], padded.shape[2] - 2, padded.shape[3] - 2
    )


def project(transfer, traction):
    return jnp.einsum("nk,ckf->ncf", transfer, traction, precision=highest).reshape(12, -1)


def local(
    face_owner,
    face_element,
    element_state,
    lift,
    face_scale,
    transfer,
    stiffness_ref,
    element_scale,
    displacement_prev,
):
    groups = lax.axis_size("grp")
    members = lax.axis_size("dev")
    devices = groups * members
    faces_dev = face_owner.shape[0]
    capacity = 2 * faces_dev // devices
    slot_total = devices * capacity
    grid_rows, grid_cols = element_scale.shape
    traces = jnp.dot(lift, element_state, preferred_element_type=jnp.float32) * face_scale[None, :]
    owners = face_owner[:, 0]
    ordering = jnp.argsort(owners, stable=True)
    sorted_owner = owners[ordering]
    firsts = jnp.searchsorted(sorted_owner, sorted_owner, side="left")
    ranked = jnp.arange(faces_dev, dtype=jnp.int32) - firsts
    slot_index = (
        jnp.zeros((faces_dev,), jnp.int32).at[ordering].set(sorted_owner * capacity + ranked)
    )
    marker = (face_element + 1).astype(jnp.float32)[None, :]
    stacked = jnp.concatenate([traces, marker], axis=0)
    outgoing = jnp.zeros((stacked.shape[0], slot_total), jnp.float32).at[:, slot_index].set(stacked)
    received = lax.all_to_all(outgoing, ("grp", "dev"), split_axis=1, concat_axis=1, tiled=True)
    marker_row = received[-1].astype(jnp.int32) - 1
    live_slot = jnp.maximum(marker_row, 0)
    values = received[:-1]
    values = project(transfer, values.reshape(3, NODES_F, -1))
    shell_load = jnp.zeros((12, grid_rows * grid_cols), jnp.float32).at[:, live_slot].add(values)
    shell_load = shell_load.reshape(4, 3, grid_rows, grid_cols)
    block_inverse = invert_block(stiffness_ref)
    stacked_block = jnp.concatenate(
        [
            displacement_prev.reshape(12, grid_rows, grid_cols),
            shell_load.reshape(12, grid_rows, grid_cols),
            element_scale[None],
        ],
        axis=0,
    )
    widened = with_halo(stacked_block, (("grp", 1), ("dev", 2)), SWEEPS)
    wide_rows = grid_rows + 2 * SWEEPS
    wide_cols = grid_cols + 2 * SWEEPS
    current = widened[:12].reshape(4, 3, wide_rows, wide_cols)
    wide_load = widened[12:24].reshape(4, 3, wide_rows, wide_cols)
    wide_scale = widened[24]
    inside = wide_scale > 0.0
    safe_scale = jnp.where(inside, wide_scale, 1.0)
    for turn_index in range(SWEEPS):
        padded = jnp.pad(current, ((0, 0), (0, 0), (1, 1), (1, 1)))
        current = jnp.where(inside, relax(padded, wide_load, block_inverse, safe_scale), 0.0)
    displacement = current[:, :, SWEEPS : SWEEPS + grid_rows, SWEEPS : SWEEPS + grid_cols]
    returning = displacement.reshape(12, -1)[:, live_slot]
    returned = lax.all_to_all(returning, ("grp", "dev"), split_axis=1, concat_axis=1, tiled=True)
    node_disp = returned[:, slot_index].reshape(4, 3, -1)
    face_displacement = jnp.einsum("nk,ncf->ckf", transfer, node_disp, precision=highest)
    return (displacement, face_displacement)


def solution(mesh):
    placed = (
        P(("grp", "dev"), None),
        P(("grp", "dev")),
        P(None, ("grp", "dev")),
        P(),
        P(("grp", "dev")),
        P(),
        P(),
        P("grp", "dev"),
        P(None, None, "grp", "dev"),
    )
    return jax.shard_map(
        local,
        mesh=mesh,
        in_specs=placed,
        out_specs=(P(None, None, "grp", "dev"), P(None, None, ("grp", "dev"))),
        check_vma=False,
    )
```

profile of v0, /device:TPU:0, one launch (start us, length us, event | category | flops | bytes accessed | tf_op | source)
XLA Modules:
  0.0 1377.4 jit_solution(13399405964006372354)
XLA Ops:
  8.0 23.0 %gather_fusion.1 = s32[4096]{0:T(1024)S(1)} fusion(s32[4096]{0:T(1024)S(1)} %bitcast.380, s32[4096]{0:T(1024)S(1)} %get-tuple-element.153), kind=kCustom, calls=%fused_computation.1 | custom fusion | bytes 49152 | tf_op jit(solution)/shard_map/gather | solution.py:89
  31.1 300.6 %while.25 = (s32[]{:T(128)}, u32[4096]{0:T(1024)S(1)}, u32[4096]{0:T(1024)S(1)}, s32[4096]{0:T(1024)S(1)}, s32[]{:T(128)}, /*index=5*/s32[]{:T(128)}, s32[]{}) while((s32[]{:T(128)}, u32[4096]{0:T(1024)S(1)}, u32[4096]{0:T(1024)S(1)}, s32[4096]{0:T(1024)S(1)}, s32[]{:T(128)}, /*index=5*/s32[]{:T(128)}, s32[]{}) %tuple.214), condition=%wide.region_2.3_spmd.clone, body=%wide.region_1.2_spmd.clone.sunk | while | flops 77828 | bytes 270437 | solution.py:90
  31.1 23.0 %gather_fusion = s32[4096]{0:T(1024)S(1)} fusion(s32[4096]{0:T(1024)S(1)} %get-tuple-element.345, u32[4096]{0:T(1024)S(1)} %broadcast_clamp_fusion.5), kind=kCustom, calls=%fused_computation.clone.clone.1 | custom fusion | bytes 49152 | tf_op jit(solution)/shard_map/jit(searchsorted)/jit(_searchsorted_scan_impl)/vmap(jit(_searchsorted_scan_impl))/while/body/eval_jaxpr/gather | solution.py:90
  54.2 23.0 %gather_fusion = s32[4096]{0:T(1024)S(1)} fusion(s32[4096]{0:T(1024)S(1)} %get-tuple-element.345, u32[4096]{0:T(1024)S(1)} %broadcast_clamp_fusion.5), kind=kCustom, calls=%fused_computation.clone.clone.1 | custom fusion | bytes 49152 | tf_op jit(solution)/shard_map/jit(searchsorted)/jit(_searchsorted_scan_impl)/vmap(jit(_searchsorted_scan_impl))/while/body/eval_jaxpr/gather | solution.py:90
  77.3 23.0 %gather_fusion = s32[4096]{0:T(1024)S(1)} fusion(s32[4096]{0:T(1024)S(1)} %get-tuple-element.345, u32[4096]{0:T(1024)S(1)} %broadcast_clamp_fusion.5), kind=kCustom, calls=%fused_computation.clone.clone.1 | custom fusion | bytes 49152 | tf_op jit(solution)/shard_map/jit(searchsorted)/jit(_searchsorted_scan_impl)/vmap(jit(_searchsorted_scan_impl))/while/body/eval_jaxpr/gather | solution.py:90
  100.5 23.0 %gather_fusion = s32[4096]{0:T(1024)S(1)} fusion(s32[4096]{0:T(1024)S(1)} %get-tuple-element.345, u32[4096]{0:T(1024)S(1)} %broadcast_clamp_fusion.5), kind=kCustom, calls=%fused_computation.clone.clone.1 | custom fusion | bytes 49152 | tf_op jit(solution)/shard_map/jit(searchsorted)/jit(_searchsorted_scan_impl)/vmap(jit(_searchsorted_scan_impl))/while/body/eval_jaxpr/gather | solution.py:90
  123.6 23.0 %gather_fusion = s32[4096]{0:T(1024)S(1)} fusion(s32[4096]{0:T(1024)S(1)} %get-tuple-element.345, u32[4096]{0:T(1024)S(1)} %broadcast_clamp_fusion.5), kind=kCustom, calls=%fused_computation.clone.clone.1 | custom fusion | bytes 49152 | tf_op jit(solution)/shard_map/jit(searchsorted)/jit(_searchsorted_scan_impl)/vmap(jit(_searchsorted_scan_impl))/while/body/eval_jaxpr/gather | solution.py:90
  146.7 23.0 %gather_fusion = s32[4096]{0:T(1024)S(1)} fusion(s32[4096]{0:T(1024)S(1)} %get-tuple-element.345, u32[4096]{0:T(1024)S(1)} %broadcast_clamp_fusion.5), kind=kCustom, calls=%fused_computation.clone.clone.1 | custom fusion | bytes 49152 | tf_op jit(solution)/shard_map/jit(searchsorted)/jit(_searchsorted_scan_impl)/vmap(jit(_searchsorted_scan_impl))/while/body/eval_jaxpr/gather | solution.py:90
  169.8 23.0 %gather_fusion = s32[4096]{0:T(1024)S(1)} fusion(s32[4096]{0:T(1024)S(1)} %get-tuple-element.345, u32[4096]{0:T(1024)S(1)} %broadcast_clamp_fusion.5), kind=kCustom, calls=%fused_computation.clone.clone.1 | custom fusion | bytes 49152 | tf_op jit(solution)/shard_map/jit(searchsorted)/jit(_searchsorted_scan_impl)/vmap(jit(_searchsorted_scan_impl))/while/body/eval_jaxpr/gather | solution.py:90
  193.0 23.0 %gather_fusion = s32[4096]{0:T(1024)S(1)} fusion(s32[4096]{0:T(1024)S(1)} %get-tuple-element.345, u32[4096]{0:T(1024)S(1)} %broadcast_clamp_fusion.5), kind=kCustom, calls=%fused_computation.clone.clone.1 | custom fusion | bytes 49152 | tf_op jit(solution)/shard_map/jit(searchsorted)/jit(_searchsorted_scan_impl)/vmap(jit(_searchsorted_scan_impl))/while/body/eval_jaxpr/gather | solution.py:90
  216.1 23.0 %gather_fusion = s32[4096]{0:T(1024)S(1)} fusion(s32[4096]{0:T(1024)S(1)} %get-tuple-element.345, u32[4096]{0:T(1024)S(1)} %broadcast_clamp_fusion.5), kind=kCustom, calls=%fused_computation.clone.clone.1 | custom fusion | bytes 49152 | tf_op jit(solution)/shard_map/jit(searchsorted)/jit(_searchsorted_scan_impl)/vmap(jit(_searchsorted_scan_impl))/while/body/eval_jaxpr/gather | solution.py:90
  239.2 23.0 %gather_fusion = s32[4096]{0:T(1024)S(1)} fusion(s32[4096]{0:T(1024)S(1)} %get-tuple-element.345, u32[4096]{0:T(1024)S(1)} %broadcast_clamp_fusion.5), kind=kCustom, calls=%fused_computation.clone.clone.1 | custom fusion | bytes 49152 | tf_op jit(solution)/shard_map/jit(searchsorted)/jit(_searchsorted_scan_impl)/vmap(jit(_searchsorted_scan_impl))/while/body/eval_jaxpr/gather | solution.py:90
  262.3 23.0 %gather_fusion = s32[4096]{0:T(1024)S(1)} fusion(s32[4096]{0:T(1024)S(1)} %get-tuple-element.345, u32[4096]{0:T(1024)S(1)} %broadcast_clamp_fusion.5), kind=kCustom, calls=%fused_computation.clone.clone.1 | custom fusion | bytes 49152 | tf_op jit(solution)/shard_map/jit(searchsorted)/jit(_searchsorted_scan_impl)/vmap(jit(_searchsorted_scan_impl))/while/body/eval_jaxpr/gather | solution.py:90
  285.5 23.0 %gather_fusion = s32[4096]{0:T(1024)S(1)} fusion(s32[4096]{0:T(1024)S(1)} %get-tuple-element.345, u32[4096]{0:T(1024)S(1)} %broadcast_clamp_fusion.5), kind=kCustom, calls=%fused_computation.clone.clone.1 | custom fusion | bytes 49152 | tf_op jit(solution)/shard_map/jit(searchsorted)/jit(_searchsorted_scan_impl)/vmap(jit(_searchsorted_scan_impl))/while/body/eval_jaxpr/gather | solution.py:90
  308.6 23.0 %gather_fusion = s32[4096]{0:T(1024)S(1)} fusion(s32[4096]{0:T(1024)S(1)} %get-tuple-element.345, u32[4096]{0:T(1024)S(1)} %broadcast_clamp_fusion.5), kind=kCustom, calls=%fused_computation.clone.clone.1 | custom fusion | bytes 49152 | tf_op jit(solution)/shard_map/jit(searchsorted)/jit(_searchsorted_scan_impl)/vmap(jit(_searchsorted_scan_impl))/while/body/eval_jaxpr/gather | solution.py:90
  331.7 15.5 %scatter_custom_fusion = s32[4096]{0:T(1024)S(1)} fusion(s32[4096]{0:T(1024)S(1)} %get-tuple-element.154, s32[4096]{0:T(1024)S(1)} %subtract_add_fusion, s32[]{:T(128)} %constant.55.clone.1), kind=kCustom, calls=%fused_computation.358 | custom fusion | bytes 16388 | tf_op jit(solution)/shard_map/scatter | solution.py:93
  348.8 12.8 scatter_custom_fusion.1
  379.9 20.3 %all-to-all-done = f32[31,32,256]{2,0,1:T(8,128)S(1)} async-done(((f32[31,32,256]{2,0,1:T(8,128)}), f32[31,32,256]{2,0,1:T(8,128)S(1)}, u32[]{:S(2)}, u32[]{:S(2)}) %all-to-all-start) | async-done | bytes 1015840 | tf_op jit(solution)/shard_map/all_to_all | solution.py:98
  407.5 56.5 %scatter_custom_fusion.2 = f32[12,16384]{0,1:T(8,128)} fusion(s32[8192]{0:T(1024)S(1)} %bitcast.413, f32[8192,12]{1,0:T(8,128)} %copy.46, f32[]{:T(128)} %constant.54.clone.1), kind=kCustom, calls=%fused_computation.14 | custom fusion | flops 98304 | bytes 786944 | tf_op jit(solution)/shard_map/scatter-add | solution.py:103
  613.6 8.6 constant_dynamic-update-slice_fusion.20
  622.2 8.4 constant_dynamic-update-slice_fusion.19
  714.9 8.6 constant_dynamic-update-slice_fusion.32
  723.5 8.4 constant_dynamic-update-slice_fusion.31
  816.2 8.6 constant_dynamic-update-slice_fusion.44
  841.6 8.7 constant_dynamic-update-slice_fusion.41
  917.9 8.6 constant_dynamic-update-slice_fusion.56
  1019.2 8.6 constant_dynamic-update-slice_fusion.68
  1120.6 8.6 constant_dynamic-update-slice_fusion.80
  1221.9 8.6 constant_dynamic-update-slice_fusion.92
  1303.6 31.3 %gather_fusion.2 = f32[8192,12]{1,0:T(8,128)} fusion(f32[12,16384]{0,1:T(8,128)} %copy.52, s32[8192]{0:T(1024)S(1)} %broadcast_clamp_fusion.1), kind=kCustom, calls=%fused_computation.2 | custom fusion | bytes 819200 | tf_op jit(solution)/shard_map/gather | solution.py:126
  1337.8 21.1 %all_to_all.21 = f32[12,32,256]{2,0,1:T(8,128)S(1)} all-to-all(f32[12,32,256]{2,0,1:T(8,128)S(1)} %copy.53), channel_id=1, replica_groups=mesh['grp'=4,'dev'=8] {'grp','dev'}, dimensions={1} | all-to-all | bytes 786432 | tf_op jit(solution)/shard_map/all_to_all | solution.py:127
  1361.5 13.0 gather_fusion.3
  (263 shorter events, 796.9 us)
Async XLA Ops:
  0.6 347.2 %copy-start = (bf16[110,4096]{1,0:T(8,128)(2,1)S(1)}, bf16[110,4096]{1,0:T(8,128)(2,1)}, u32[]{:S(2)}) copy-start(bf16[110,4096]{1,0:T(8,128)(2,1)} %param.13) | copy-start | bytes 2703364
  0.6 7.3 copy-start.2
  31.0 316.8 %copy-start.14 = (f32[4096]{0:T(1024)S(1)}, f32[4096]{0:T(1024)}, u32[]{:S(2)}) copy-start(f32[4096]{0:T(1024)} %param.15) | copy-start | bytes 49156
  31.0 316.8 %copy-start.15 = (bf16[30,110]{1,0:T(8,128)(2,1)S(1)}, bf16[30,110]{1,0:T(8,128)(2,1)}, u32[]{:S(2)}) copy-start(bf16[30,110]{1,0:T(8,128)(2,1)} %param.14) | copy-start | bytes 19804
  365.3 7.5 copy-start.12
  365.3 35.0 %all-to-all-start = ((f32[31,32,256]{2,0,1:T(8,128)}), f32[31,32,256]{2,0,1:T(8,128)S(1)}, u32[]{:S(2)}, u32[]{:S(2)}) async-start(f32[31,32,256]{2,0,1:T(8,128)} %copy.43), calls=%async_computation | async-start | bytes 2097152 | tf_op jit(solution)/shard_map/all_to_all | solution.py:98
  401.8 1.4 copy-start.16
  464.0 5.4 copy-start.3
  464.0 5.4 copy-start.10
  469.4 6.7 collective-permute-start
  470.7 10.1 collective-permute-start.1
  476.1 17.1 %copy-start.5 = (f32[25,8,256]{2,1,0:T(8,128)}, f32[25,8,256]{2,1,0:T(8,128)S(1)}, u32[]{:S(2)}) copy-start(f32[25,8,256]{2,1,0:T(8,128)S(1)} %collective-permute-done) | copy-start | bytes 614404
  480.8 12.4 copy-start.7
  484.1 6.7 collective-permute-start.3
  485.4 4.1 collective-permute-start.2
  492.1 1.2 copy-start.4
  494.5 0.9 copy-start.6
  494.5 1.0 copy-start.8
  494.5 1.0 copy-start.11
  1298.0 0.9 copy-start.9
  1358.8 2.6 copy-start.13
  1374.5 2.8 copy-start.1
where the time goes:
time: 1390 us; the launch traced here: 1380 us
  other arithmetic  870 us (63%)
  local copies, waits for them, and re-layouts  437 us (31%)
  waiting for transfers between devices  27.9 us (2%)
  blocking collectives  21.1 us (2%)
  starting transfers between devices  15.3 us (1%)
    unnamed x90, other arithmetic  724 us
    gather x13, local copies, waits for them, and re-layouts, local(): firsts = jnp.searchsorted(sorted_owner, sorted_owner, side='left')  299 us
    another operation x8, other arithmetic, relax(): jnp.stack(outputs)  63.3 us
    scatter-add x1, other arithmetic, local(): jnp.zeros((12, grid_rows * grid_cols), jnp.float32).at[:, live_slot]  56.5 us
    gather x1, local copies, waits for them, and re-layouts, local(): returning = displacement.reshape(12, -1)[:, live_slot]  31.3 us
  transfers between devices with their start and end apart: 5, of which 4 were waited for; matrix products, arithmetic and copies ran while one was open for 1% of the time, Pallas kernels for 0%

commit v1 on v0

v1 whole, which is shorter than its diff:
```python
import functools

import jax
import jax.numpy as jnp
from jax import lax
from jax.experimental import pallas as pl
from jax.experimental.pallas import tpu as pltpu
from jax.sharding import PartitionSpec as P

NODES_F = 10
SWEEPS = 8
LANES = 128

coupling_weight = 2.2
highest = lax.Precision.HIGHEST
F32 = jnp.float32
BF16 = jnp.bfloat16
NT = (((1,), (1,)), ((), ()))
VM = pl.BlockSpec(memory_space=pltpu.VMEM)
SM = pl.BlockSpec(memory_space=pltpu.SMEM)


def split(x):
    high = x.astype(BF16).astype(F32)
    return high, x - high


def one_hot(row, count):
    places = lax.broadcasted_iota(jnp.int32, (count, row.shape[1]), 0).astype(F32)
    return jnp.where(places == row, 1.0, 0.0).astype(BF16)


def route_kernel(n, cap, cols, owner_ref, element_ref, state_ref, lift_ref, scale_ref, spread_ref,
                 stiff_ref, out_ref, rank_ref, inverse_ref, counts):
    step = pl.program_id(0)
    width = owner_ref.shape[1]

    @pl.when(step == 0)
    def _():
        out_ref[...] = jnp.zeros_like(out_ref)
        counts[...] = jnp.zeros_like(counts)
        stiffness = stiff_ref[...]
        identity = (
            lax.broadcasted_iota(jnp.int32, (12, 12), 0)
            == lax.broadcasted_iota(jnp.int32, (12, 12), 1)
        ).astype(F32)
        approx = identity / 5.0
        for _ in range(8):
            product = jnp.dot(stiffness, approx, precision=highest, preferred_element_type=F32)
            approx = jnp.dot(
                approx, 2.0 * identity - product, precision=highest, preferred_element_type=F32
            )
        inverse_ref[...] = approx

    owner = owner_ref[...]
    owner_f = owner.astype(F32)
    traces = jnp.dot(lift_ref[...], state_ref[...], preferred_element_type=F32) * scale_ref[...]
    loads = jnp.dot(spread_ref[...], traces, precision=highest, preferred_element_type=F32)
    element = element_ref[...]
    high_row = (element // cols).astype(F32)
    low_row = (element % cols).astype(F32)
    where_row = lax.broadcasted_iota(jnp.int32, loads.shape, 0)
    values = jnp.where(where_row == 12, high_row, jnp.where(where_row == 13, low_row, loads))

    owner_hot = one_hot(owner_f, n)
    before = (
        lax.broadcasted_iota(jnp.int32, (width, width), 0)
        < lax.broadcasted_iota(jnp.int32, (width, width), 1)
    ).astype(F32).astype(BF16)
    running = jnp.dot(owner_hot, before, preferred_element_type=F32) + counts[:, :1]
    hot = owner_hot.astype(F32)
    rank = jnp.sum(hot * running, axis=0, keepdims=True)
    rank_ref[...] = rank
    counts[...] = counts[...] + jnp.sum(hot, axis=1, keepdims=True)

    slot_hot = one_hot(rank, cap)
    high, low = split(values)
    owner_wide = jnp.broadcast_to(owner, values.shape)
    highs, lows = [], []
    for d in range(n):
        mine = owner_wide == d
        highs.append(jnp.where(mine, high, 0.0).astype(BF16))
        lows.append(jnp.where(mine, low, 0.0).astype(BF16))
    left = jnp.concatenate(
        [jnp.concatenate(highs, axis=0), jnp.concatenate(lows, axis=0)], axis=1
    )
    right = jnp.concatenate([slot_hot, slot_hot], axis=1)
    out_ref[...] += lax.dot_general(left, right, NT, preferred_element_type=F32)


def route(n, cap, cols, owner, element, state, lift, scale, spread, stiffness):
    faces = owner.shape[1]
    width = 512
    whole = lambda a: pl.BlockSpec(a.shape, lambda i: (0,) * a.ndim)
    row = pl.BlockSpec((1, width), lambda i: (0, i))
    return pl.pallas_call(
        functools.partial(route_kernel, n, cap, cols),
        grid=(faces // width,),
        in_specs=[row, row, pl.BlockSpec((state.shape[0], width), lambda i: (0, i)), whole(lift),
                  row, whole(spread), whole(stiffness)],
        out_specs=[pl.BlockSpec((n * 16, cap), lambda i: (0, 0)), row,
                   pl.BlockSpec((12, 12), lambda i: (0, 0))],
        out_shape=[jax.ShapeDtypeStruct((n * 16, cap), F32),
                   jax.ShapeDtypeStruct((1, faces), F32),
                   jax.ShapeDtypeStruct((12, 12), F32)],
        scratch_shapes=[pltpu.VMEM((n, LANES), F32)],
        name="route",
    )(owner, element, state, lift, scale, spread, stiffness)


def lanes_of(ref):
    return jnp.concatenate([ref[g] for g in range(ref.shape[0])], axis=1)


def gather_kernel_in(rows, cols, recv_ref, prev_ref, scale_ref, load_ref, edge_ref, strip_ref):
    step = pl.program_id(0)

    @pl.when(step == 0)
    def _():
        load_ref[...] = jnp.zeros_like(load_ref)

    values = lanes_of(recv_ref)
    width = values.shape[1]
    mask = lax.broadcasted_iota(jnp.int32, (rows, width), 0).astype(F32) == values[12:13]
    low_hot = one_hot(values[13:14], cols)
    high, low = split(values)
    highs, lows = [], []
    for c in range(12):
        highs.append(jnp.where(mask, high[c : c + 1], 0.0).astype(BF16))
        lows.append(jnp.where(mask, low[c : c + 1], 0.0).astype(BF16))
    left = jnp.concatenate(
        [jnp.concatenate(highs, axis=0), jnp.concatenate(lows, axis=0)], axis=1
    )
    right = jnp.concatenate([low_hot, low_hot], axis=1)
    total = lax.dot_general(left, right, NT, preferred_element_type=F32)
    load_ref[...] += total.reshape(12, rows, cols)

    @pl.when(step == pl.num_programs(0) - 1)
    def _():
        scale = scale_ref[...]
        for side, start in ((0, 0), (1, rows - SWEEPS)):
            edge_ref[side, :12] = prev_ref[:, start : start + SWEEPS, :]
            edge_ref[side, 12] = scale[start : start + SWEEPS]
            edge_ref[side, 13:] = load_ref[:, start : start + SWEEPS, :]
        lane = lax.broadcasted_iota(jnp.int32, (rows, LANES), 1) // SWEEPS
        for side in range(2):
            base = 0 if side == 0 else cols - LANES
            turn = 0 if side == 0 else SWEEPS
            for kind in range(2):
                pieces = [(prev_ref if kind == 0 else load_ref)[c, :, base : base + LANES] for c in range(12)]
                if kind == 0:
                    pieces.append(scale[:, base : base + LANES])
                packed = jnp.zeros((rows, LANES), F32)
                for j, piece in enumerate(pieces):
                    move = (j * SWEEPS + turn) % LANES
                    piece = pltpu.roll(piece, move, 1) if move else piece
                    packed = jnp.where(lane == j, piece, packed)
                strip_ref[side, kind] = packed


def collect(rows, cols, recv, prev, scale):
    groups, _, cap = recv.shape
    block = max(1, min(groups, 1024 // cap))
    whole = lambda shape: pl.BlockSpec(shape, lambda i: (0,) * len(shape))
    shapes = [(12, rows, cols), (2, 25, SWEEPS, cols), (2, 2, rows, LANES)]
    return pl.pallas_call(
        functools.partial(gather_kernel_in, rows, cols),
        grid=(groups // block,),
        in_specs=[pl.BlockSpec((block, 16, cap), lambda i: (i, 0, 0)), whole(prev.shape),
                  whole(scale.shape)],
        out_specs=[whole(s) for s in shapes],
        out_shape=[jax.ShapeDtypeStruct(s, F32) for s in shapes],
        name="collect",
    )(recv, prev, scale)


def exchange(edge, strip, rows):
    groups, members = lax.axis_size("grp"), lax.axis_size("dev")

    def move(x, up, right):
        pairs = []
        for g in range(groups):
            for d in range(members):
                if 0 <= g + up < groups and 0 <= d + right < members:
                    pairs.append((g * members + d, (g + up) * members + d + right))
        return lax.ppermute(x, ("grp", "dev"), pairs)

    edges = jnp.stack([move(edge[1], 1, 0), move(edge[0], -1, 0)])
    strips = jnp.stack([move(strip[1], 0, 1), move(strip[0], 0, -1)])
    corners = jnp.stack([
        jnp.stack([move(strip[1][:, rows - SWEEPS :], 1, 1), move(strip[0][:, rows - SWEEPS :], 1, -1)]),
        jnp.stack([move(strip[1][:, :SWEEPS], -1, 1), move(strip[0][:, :SWEEPS], -1, -1)]),
    ])
    return edges, strips, corners


def sweep_kernel(rows, cols, prev_ref, load_ref, scale_ref, edge_ref, strip_ref, corner_ref,
                 inverse_ref, out_ref, one, two, base, factor):
    top = 2 * SWEEPS
    wide = cols + LANES
    tall = rows + 2 * top
    zero_rows = jnp.zeros((12, SWEEPS, wide), F32)
    for start in (0, tall - SWEEPS):
        one[:, start : start + SWEEPS, :] = zero_rows
        two[:, start : start + SWEEPS, :] = zero_rows
    one[:, top : top + rows, :cols] = prev_ref[...]
    base[:, top : top + rows, :cols] = load_ref[...]
    factor[top : top + rows, :cols] = scale_ref[...]
    for side, start in ((0, top - SWEEPS), (1, top + rows)):
        one[:, start : start + SWEEPS, :cols] = edge_ref[side, :12]
        base[:, start : start + SWEEPS, :cols] = edge_ref[side, 13:]
        factor[start : start + SWEEPS, :cols] = edge_ref[side, 12]

    def unpack(west, east, start, kind):
        size = west.shape[0]
        lane = lax.broadcasted_iota(jnp.int32, (size, LANES), 1)
        for j in range(13 if kind == 0 else 12):
            back = (LANES - j * SWEEPS) % LANES
            first = pltpu.roll(east, back, 1) if back else east
            back = (back - SWEEPS) % LANES
            last = pltpu.roll(west, back, 1) if back else west
            piece = jnp.where(lane < SWEEPS, first, jnp.where(lane >= LANES - SWEEPS, last, 0.0))
            if j == 12:
                factor[start : start + size, cols:] = piece
            elif kind == 0:
                one[j, start : start + size, cols:] = piece
            else:
                base[j, start : start + size, cols:] = piece

    for kind in range(2):
        unpack(strip_ref[0, kind], strip_ref[1, kind], top, kind)
        for side, start in ((0, top - SWEEPS), (1, top + rows)):
            unpack(corner_ref[side, 0, kind], corner_ref[side, 1, kind], start, kind)

    starts = list(range(top - SWEEPS, top + rows + SWEEPS, 8))
    for start in starts:
        here = slice(start, start + 8)
        scale = factor[here, :]
        inside = scale > 0.0
        inv = jnp.where(inside, 1.0 / jnp.where(inside, scale, 1.0), 0.0)
        loads = [base[j, here, :] for j in range(12)]
        for i in range(12):
            total = inverse_ref[i, 0] * loads[0]
            for j in range(1, 12):
                total = total + inverse_ref[i, j] * loads[j]
            base[i, here, :] = total * inv
        factor[here, :] = inv * coupling_weight

    def relax(source, target, wanted):
        for start in wanted:
            here = slice(start, start + 8)
            south = slice(start - 1, start + 7)
            north = slice(start + 1, start + 9)
            sources = []
            for node, (turn, beside, rows_at, below) in enumerate(
                ((1, 1, south, 2), (wide - 1, 0, south, 3), (1, 3, north, 0), (wide - 1, 2, north, 1))
            ):
                for c in range(3):
                    sources.append(
                        pltpu.roll(source[3 * beside + c, here, :], turn, 1)
                        + source[3 * below + c, rows_at, :]
                    )
            inv = factor[here, :]
            for i in range(12):
                total = inverse_ref[i, 0] * sources[0]
                for j in range(1, 12):
                    total = total + inverse_ref[i, j] * sources[j]
                target[i, here, :] = base[i, here, :] + total * inv

    def pair(_, carry):
        relax(one, two, starts)
        relax(two, one, starts)
        return carry

    lax.fori_loop(0, SWEEPS // 2, pair, 0)
    out_ref[...] = one[:, top : top + rows, :cols]


def sweep(rows, cols, prev, load, scale, edges, strips, corners, inverse):
    tall, wide = rows + 4 * SWEEPS, cols + LANES
    return pl.pallas_call(
        functools.partial(sweep_kernel, rows, cols),
        in_specs=[VM] * 6 + [SM],
        out_specs=VM,
        out_shape=jax.ShapeDtypeStruct((12, rows, cols), F32),
        scratch_shapes=[pltpu.VMEM((12, tall, wide), F32)] * 3 + [pltpu.VMEM((tall, wide), F32)],
        name="sweep",
    )(prev, load, scale, edges, strips, corners, inverse)


def answer_kernel(rows, cols, disp_ref, recv_ref, out_ref, table):
    @pl.when(pl.program_id(0) == 0)
    def _():
        high, low = split(disp_ref[...].reshape(12 * rows, cols))
        table[...] = jnp.concatenate([high.astype(BF16), low.astype(BF16)], axis=1)

    values = lanes_of(recv_ref)
    width = values.shape[1]
    cap = recv_ref.shape[2]
    mask = lax.broadcasted_iota(jnp.int32, (rows, width), 0).astype(F32) == values[12:13]
    low_hot = one_hot(values[13:14], cols)
    picked = jnp.dot(
        table[...], jnp.concatenate([low_hot, low_hot], axis=0), preferred_element_type=F32
    )
    lines = [
        jnp.sum(jnp.where(mask, picked[c * rows : (c + 1) * rows], 0.0), axis=0, keepdims=True)
        for c in range(12)
    ]
    result = jnp.concatenate(lines + [jnp.zeros((4, width), F32)], axis=0)
    for g in range(recv_ref.shape[0]):
        out_ref[g] = result[:, g * cap : (g + 1) * cap]


def answer(rows, cols, disp, recv):
    groups, _, cap = recv.shape
    block = max(1, min(groups, 1024 // cap))
    spec = pl.BlockSpec((block, 16, cap), lambda i: (i, 0, 0))
    return pl.pallas_call(
        functools.partial(answer_kernel, rows, cols),
        grid=(groups // block,),
        in_specs=[pl.BlockSpec(disp.shape, lambda i: (0, 0, 0)), spec],
        out_specs=spec,
        out_shape=jax.ShapeDtypeStruct(recv.shape, F32),
        scratch_shapes=[pltpu.VMEM((12 * rows, 2 * cols), BF16)],
        name="answer",
    )(disp, recv)


def finish_kernel(n, cap, back_ref, owner_ref, rank_ref, spread_ref, out_ref, table):
    @pl.when(pl.program_id(0) == 0)
    def _():
        high, low = split(back_ref[...])
        table[...] = jnp.concatenate([high.astype(BF16), low.astype(BF16)], axis=1)

    slot_hot = one_hot(rank_ref[...], cap)
    picked = jnp.dot(
        table[...], jnp.concatenate([slot_hot, slot_hot], axis=0), preferred_element_type=F32
    )
    width = owner_ref.shape[1]
    owner = jnp.broadcast_to(owner_ref[...], (16, width))
    node = jnp.zeros((16, width), F32)
    for d in range(n):
        node = jnp.where(owner == d, picked[d * 16 : (d + 1) * 16], node)
    for c in range(3):
        out_ref[c] = jnp.dot(spread_ref[c], node, precision=highest, preferred_element_type=F32)


def finish(n, cap, back, owner, rank, spread):
    faces = owner.shape[1]
    width = 512
    row = pl.BlockSpec((1, width), lambda i: (0, i))
    return pl.pallas_call(
        functools.partial(finish_kernel, n, cap),
        grid=(faces // width,),
        in_specs=[pl.BlockSpec((n * 16, cap), lambda i: (0, 0)), row, row,
                  pl.BlockSpec(spread.shape, lambda i: (0, 0, 0))],
        out_specs=pl.BlockSpec((3, NODES_F, width), lambda i: (0, 0, i)),
        out_shape=jax.ShapeDtypeStruct((3, NODES_F, faces), F32),
        scratch_shapes=[pltpu.VMEM((n * 16, 2 * cap), BF16)],
        name="finish",
    )(back, owner, rank, spread)


def swap(x):
    return lax.all_to_all(x, ("grp", "dev"), split_axis=0, concat_axis=0, tiled=True)


def local(
    face_owner,
    face_element,
    element_state,
    lift,
    face_scale,
    transfer,
    stiffness_ref,
    element_scale,
    displacement_prev,
):
    n = lax.axis_size("grp") * lax.axis_size("dev")
    faces = face_owner.shape[0]
    cap = 2 * faces // n
    rows, cols = element_scale.shape
    prev = displacement_prev.reshape(12, rows, cols)
    owner = face_owner.reshape(1, faces)
    spread = jnp.einsum("nk,cd->ncdk", transfer, jnp.eye(3, dtype=F32), precision=highest)
    spread_in = jnp.pad(spread.reshape(12, 3 * NODES_F), ((0, 4), (0, 0)))
    spread_out = jnp.pad(spread.transpose(2, 3, 0, 1).reshape(3, NODES_F, 12), ((0, 0), (0, 0), (0, 4)))
    outgoing, rank, inverse = route(
        n, cap, cols, owner, face_element.reshape(1, faces), element_state, lift,
        face_scale.reshape(1, faces), spread_in, stiffness_ref,
    )
    received = swap(outgoing.reshape(n, 16, cap))
    fold = max(1, LANES // cap)
    if fold > 1:
        received = received.reshape(n // fold, fold, 16, cap).transpose(0, 2, 1, 3)
        received = received.reshape(n // fold, 16, fold * cap)
    load, edge, strip = collect(rows, cols, received, prev, element_scale)
    edges, strips, corners = exchange(edge, strip, rows)
    disp = sweep(rows, cols, prev, load, element_scale, edges, strips, corners, inverse)
    returning = answer(rows, cols, disp, received)
    if fold > 1:
        returning = returning.reshape(n // fold, 16, fold, cap).transpose(0, 2, 1, 3)
        returning = returning.reshape(n, 16, cap)
    back = swap(returning).reshape(n * 16, cap)
    face_displacement = finish(n, cap, back, owner, rank, spread_out)
    return (disp.reshape(4, 3, rows, cols), face_displacement)


def solution(mesh):
    placed = (
        P(("grp", "dev"), None),
        P(("grp", "dev")),
        P(None, ("grp", "dev")),
        P(),
        P(("grp", "dev")),
        P(),
        P(),
        P("grp", "dev"),
        P(None, None, "grp", "dev"),
    )
    return jax.shard_map(
        local,
        mesh=mesh,
        in_specs=placed,
        out_specs=(P(None, None, "grp", "dev"), P(None, None, ("grp", "dev"))),
        check_vma=False,
    )
```

time: 1390 us -> 140 us (0.10)
  other arithmetic: 870 us -> 2.16 us
  local copies, waits for them, and re-layouts: 437 us -> 7.14 us
  Pallas kernels: 0 us -> 57.4 us
    unnamed x90 -> x0, other arithmetic: 724 us -> none
    gather x17 -> x0, local copies, waits for them, and re-layouts: 367 us -> none  [the longest x13 299 us: local(): firsts = jnp.searchsorted(sorted_owner, sorted_owner, side='left')]
    another operation x8 -> x6, other arithmetic: 63.3 us -> 2.09 us  [the longest x1 0.79 us: exchange(): edges = jnp.stack([move(edge[1], 1, 0), move(edge[0], -1, 0)])]
    pallas_call x0 -> x5, Pallas kernels: none -> 57.4 us  [the longest x1 17.6 us: sweep(): pl.pallas_call(functools.partial(sweep_kernel, rows, cols), in_specs=[VM]...]
    scatter-add x1 -> x0, other arithmetic: 56.5 us -> none  [local(): jnp.zeros((12, grid_rows * grid_cols), jnp.float32).at[:, live_slot]]
    scatter x2 -> x0, local copies, waits for them, and re-layouts: 28.3 us -> none  [the longest x1 15.5 us: local(): jnp.zeros((faces_dev,), jnp.int32).at[ordering]]
  transfers between devices with their start and end apart: 5 -> 9, of which waited for: 4 -> 3; matrix products, arithmetic and copies ran while one was open for 1% -> 2% of each run, Pallas kernels for 0% -> 0%
where the time goes in v1:
time: 140 us; the launch traced here: 139 us
  Pallas kernels  57.4 us (41%)
  waiting for transfers between devices  25.8 us (18%)
  blocking collectives  23.7 us (17%)
  starting transfers between devices  22.4 us (16%)
  local copies, waits for them, and re-layouts  7.14 us (5%)
  other arithmetic  2.16 us (2%)
    all_to_all x1, blocking collectives, swap(): lax.all_to_all(x, ('grp', 'dev'), split_axis=0, concat_axis=0, tiled=True)  23.7 us
    ppermute x8, starting transfers between devices, move(): return lax.ppermute(x, ('grp', 'dev'), pairs)  19.8 us
    pallas_call x1, Pallas kernels, sweep(): pl.pallas_call(functools.partial(sweep_kernel, rows, cols), in_specs=[VM]...  17.6 us
    all_to_all x1, waiting for transfers between devices, swap(): lax.all_to_all(x, ('grp', 'dev'), split_axis=0, concat_axis=0, tiled=True)  15.5 us
    pallas_call x1, Pallas kernels, route(): pl.pallas_call(functools.partial(route_kernel, n, cap, cols), grid=(faces...  11.3 us
    pallas_call x1, Pallas kernels, collect(): pl.pallas_call(functools.partial(gather_kernel_in, rows, cols), grid=(gro...  11.1 us
    ppermute x8, waiting for transfers between devices, move(): return lax.ppermute(x, ('grp', 'dev'), pairs)  10.3 us
    pallas_call x1, Pallas kernels, answer(): pl.pallas_call(functools.partial(answer_kernel, rows, cols), grid=(groups...  10.1 us
  transfers between devices with their start and end apart: 9, of which 3 were waited for; matrix products, arithmetic and copies ran while one was open for 2% of the time, Pallas kernels for 0%

profile of v1, /device:TPU:0, one launch (start us, length us, event | category | flops | bytes accessed | tf_op | source)
XLA Modules:
  0.0 139.5 jit_solution(17940758086839858124)
XLA Ops:
  0.7 0.7 copy-done.1
  1.3 0.1 broadcast_multiply_fusion
  1.4 0.1 reshape.35
  1.5 0.6 pad.8.spread_ref
  2.1 11.3 %route.1 = (f32[512,256]{1,0:T(8,128)}, f32[1,4096]{1,0:T(1,128)}, f32[12,12]{1,0:T(8,128)}) custom-call(s32[1,4096]{1,0:T(1,128)} %bitcast.40, s32[1,4096]{1,0:T(1,128)} %bitcast.44, bf16[110,4096]{1,0:T(8,128)(2,1)} %state_ref.1, bf16[30,110]{1,0:T(8,128)(2,1)} %lift_ref.1, f32[1,4096]{1,0:T(1,128)} %bitcast.45, f32[16,30]{1,0:T(8,128)} %pad.8.spread_ref, ...), custom_call_target="tpu_custom_call" | custom-call | tf_op jit(solution)/shard_map/route/pallas_call | solution.py:96
  13.3 23.7 %all_to_all.10.recv_ref = f32[32,16,256]{2,1,0:T(8,128)} all-to-all(f32[32,16,256]{2,1,0:T(8,128)} %bitcast.36), channel_id=1, replica_groups=mesh['grp'=4,'dev'=8] {'grp','dev'}, dimensions={0} | all-to-all | bytes 1048576 | tf_op jit(solution)/shard_map/all_to_all | solution.py:365
  37.0 11.1 %collect.1 = (f32[12,64,256]{2,1,0:T(8,128)}, f32[2,25,8,256]{3,2,1,0:T(8,128)}, f32[2,2,64,128]{3,2,1,0:T(8,128)}) custom-call(f32[32,16,256]{2,1,0:T(8,128)} %all_to_all.10.recv_ref, f32[12,64,256]{2,1,0:T(8,128)} %bitcast.33, f32[64,256]{1,0:T(8,128)} %scale_ref.3), custom_call_target="tpu_custom_call" | custom-call | tf_op jit(solution)/shard_map/collect/pallas_call | solution.py:166
  48.1 0.9 slice_bitcast_fusion.3
  49.0 2.0 %collective-permute-start.2 = (f32[2,64,128]{2,1,0:T(8,128)S(1)}, f32[2,64,128]{2,1,0:T(8,128)S(1)}, u32[]{:S(2)}, u32[]{:S(2)}) collective-permute-start(f32[2,64,128]{2,1,0:T(8,128)S(1)} %get-tuple-element.20), channel_id=1, source_target_pairs={{0,1},{1,2},{2,3},{3,4},{4,5},{5,6},{6,7},{8,9},{9,10},{10,11},{11... | collective-permute-start | bytes 196616 | tf_op jit(solution)/shard_map/ppermute | solution.py:186
  51.0 1.3 collective-permute-start.3
  52.3 0.7 collective-permute-start.5
  53.0 1.3 collective-permute-start.7
  54.3 5.8 %collective-permute-start.4 = (f32[2,8,128]{2,1,0:T(8,128)S(1)}, f32[2,8,128]{2,1,0:T(8,128)S(1)}, u32[]{:S(2)}, u32[]{:S(2)}) collective-permute-start(f32[2,8,128]{2,1,0:T(8,128)S(1)} %get-tuple-element.22), channel_id=1, source_target_pairs={{0,9},{1,10},{2,11},{3,12},{4,13},{5,14},{6,15},{8,17},{9,18},{10,... | collective-permute-start | bytes 24584 | tf_op jit(solution)/shard_map/ppermute | solution.py:186
  60.1 1.1 slice_bitcast_fusion.1
  61.2 0.0 collective-permute-done.5
  61.2 0.7 collective-permute-start.6
  61.9 6.8 %collective-permute-start = (f32[25,8,256]{2,1,0:T(8,128)S(1)}, f32[25,8,256]{2,1,0:T(8,128)S(1)}, u32[]{:S(2)}, u32[]{:S(2)}) collective-permute-start(f32[25,8,256]{2,1,0:T(8,128)S(1)} %get-tuple-element.18), channel_id=1, source_target_pairs={{0,8},{1,9},{2,10},{3,11},{4,12},{5,13},{6,14},{7,15},{8,16},{9,17... | collective-permute-start | bytes 614408 | tf_op jit(solution)/shard_map/ppermute | solution.py:186
  68.7 1.3 collective-permute-start.1
  70.0 0.6 pad_maximum_fusion.2.corner_ref
  70.7 0.7 pad_maximum_fusion.1.strip_ref
  71.3 2.5 %collective-permute-done = f32[25,8,256]{2,1,0:T(8,128)S(1)} collective-permute-done((f32[25,8,256]{2,1,0:T(8,128)S(1)}, f32[25,8,256]{2,1,0:T(8,128)S(1)}, u32[]{:S(2)}, u32[]{:S(2)}) %collective-permute-start) | collective-permute-done | bytes 204832 | tf_op jit(solution)/shard_map/ppermute | solution.py:186
  73.8 7.8 %collective-permute-done.1 = f32[25,8,256]{2,1,0:T(8,128)S(1)} collective-permute-done((f32[25,8,256]{2,1,0:T(8,128)S(1)}, f32[25,8,256]{2,1,0:T(8,128)S(1)}, u32[]{:S(2)}, u32[]{:S(2)}) %collective-permute-start.1) | collective-permute-done | bytes 204832 | tf_op jit(solution)/shard_map/ppermute | solution.py:186
  81.6 0.8 pad_maximum_fusion.edge_ref
  82.4 17.6 %sweep.1.disp_ref = f32[12,64,256]{2,1,0:T(8,128)} custom-call(f32[12,64,256]{2,1,0:T(8,128)} %bitcast.34, f32[12,64,256]{2,1,0:T(8,128)} %get-tuple-element.9.load_ref, f32[64,256]{1,0:T(8,128)} %scale_ref.3, f32[2,25,8,256]{3,2,1,0:T(8,128)} %pad_maximum_fusion.edge_ref, f32[2,2,64,128]{3,2,1,0:T(8,128)} %pad_maximum_fusion.1.strip_ref, ...), custom_call_target="tpu_custom_call" | custom-call | tf_op jit(solution)/shard_map/sweep/pallas_call | solution.py:281
  100.0 10.1 %answer.1 = f32[32,16,256]{2,1,0:T(8,128)} custom-call(f32[12,64,256]{2,1,0:T(8,128)} %sweep.1.disp_ref, f32[32,16,256]{2,1,0:T(8,128)} %all_to_all.10.recv_ref), custom_call_target="tpu_custom_call" | custom-call | tf_op jit(solution)/shard_map/answer/pallas_call | solution.py:318
  110.1 2.6 %all-to-all-start.1 = ((f32[32,16,256]{2,1,0:T(8,128)}), f32[32,16,256]{2,1,0:T(8,128)S(1)}, u32[]{:S(2)}, u32[]{:S(2)}) async-start(f32[32,16,256]{2,1,0:T(8,128)} %answer.1), calls=%async_computation.1 | async-start | bytes 1048576 | tf_op jit(solution)/shard_map/all_to_all | solution.py:365
  112.8 0.1 copy.14
  112.9 0.6 pad.9.spread_ref
  113.5 15.5 %all-to-all-done.1 = f32[32,16,256]{2,1,0:T(8,128)S(1)} async-done(((f32[32,16,256]{2,1,0:T(8,128)}), f32[32,16,256]{2,1,0:T(8,128)S(1)}, u32[]{:S(2)}, u32[]{:S(2)}) %all-to-all-start.1) | async-done | bytes 524320 | tf_op jit(solution)/shard_map/all_to_all | solution.py:365
  129.0 0.8 copy-done
  129.8 7.4 %finish.1 = f32[3,10,4096]{2,1,0:T(8,128)} custom-call(f32[512,256]{1,0:T(8,128)} %bitcast.35, s32[1,4096]{1,0:T(1,128)} %bitcast.41, f32[1,4096]{1,0:T(1,128)} %get-tuple-element.13.rank_ref, f32[3,10,16]{2,1,0:T(8,128)} %pad.9.spread_ref), custom_call_target="tpu_custom_call" | custom-call | tf_op jit(solution)/shard_map/finish/pallas_call | solution.py:352
  137.2 2.3 %copy.15 = f32[3,10,4096]{2,0,1:T(4,128)} copy(f32[3,10,4096]{2,1,0:T(8,128)} %finish.1) | data formatting | bytes 983040
  (12 shorter events, 0.0 us)
Async XLA Ops:
  0.6 0.7 copy-start.1
  49.0 21.7 %collective-permute-start.2 = (f32[2,64,128]{2,1,0:T(8,128)S(1)}, f32[2,64,128]{2,1,0:T(8,128)S(1)}, u32[]{:S(2)}, u32[]{:S(2)}) collective-permute-start(f32[2,64,128]{2,1,0:T(8,128)S(1)} %get-tuple-element.20), channel_id=1, source_target_pairs={{0,1},{1,2},{2,3},{3,4},{4,5},{5,6},{6,7},{8,9},{9,10},{10,11},{11... | collective-permute-start | bytes 196616 | tf_op jit(solution)/shard_map/ppermute | solution.py:186
  51.0 19.6 %collective-permute-start.3 = (f32[2,64,128]{2,1,0:T(8,128)S(1)}, f32[2,64,128]{2,1,0:T(8,128)S(1)}, u32[]{:S(2)}, u32[]{:S(2)}) collective-permute-start(f32[2,64,128]{2,1,0:T(8,128)S(1)} %get-tuple-element.21), channel_id=1, source_target_pairs={{1,0},{2,1},{3,2},{4,3},{5,4},{6,5},{7,6},{9,8},{10,9},{11,10},{12... | collective-permute-start | bytes 196616 | tf_op jit(solution)/shard_map/ppermute | solution.py:186
  52.3 8.8 %collective-permute-start.5 = (f32[2,8,128]{2,1,0:T(8,128)S(1)}, f32[2,8,128]{2,1,0:T(8,128)S(1)}, u32[]{:S(2)}, u32[]{:S(2)}) collective-permute-start(f32[2,8,128]{2,1,0:T(8,128)S(1)} %get-tuple-element.24), channel_id=1, source_target_pairs={{1,8},{2,9},{3,10},{4,11},{5,12},{6,13},{7,14},{9,16},{10,17},{11,... | collective-permute-start | bytes 24584 | tf_op jit(solution)/shard_map/ppermute | solution.py:186
  53.0 15.7 %collective-permute-start.7 = (f32[2,8,128]{2,1,0:T(8,128)S(1)}, f32[2,8,128]{2,1,0:T(8,128)S(1)}, u32[]{:S(2)}, u32[]{:S(2)}) collective-permute-start(f32[2,8,128]{2,1,0:T(8,128)S(1)} %get-tuple-element.25), channel_id=1, source_target_pairs={{9,0},{10,1},{11,2},{12,3},{13,4},{14,5},{15,6},{17,8},{18,9},{19,... | collective-permute-start | bytes 24584 | tf_op jit(solution)/shard_map/ppermute | solution.py:186
  54.3 7.5 %collective-permute-start.4 = (f32[2,8,128]{2,1,0:T(8,128)S(1)}, f32[2,8,128]{2,1,0:T(8,128)S(1)}, u32[]{:S(2)}, u32[]{:S(2)}) collective-permute-start(f32[2,8,128]{2,1,0:T(8,128)S(1)} %get-tuple-element.22), channel_id=1, source_target_pairs={{0,9},{1,10},{2,11},{3,12},{4,13},{5,14},{6,15},{8,17},{9,18},{10,... | collective-permute-start | bytes 24584 | tf_op jit(solution)/shard_map/ppermute | solution.py:186
  61.2 8.8 %collective-permute-start.6 = (f32[2,8,128]{2,1,0:T(8,128)S(1)}, f32[2,8,128]{2,1,0:T(8,128)S(1)}, u32[]{:S(2)}, u32[]{:S(2)}) collective-permute-start(f32[2,8,128]{2,1,0:T(8,128)S(1)} %get-tuple-element.23), channel_id=1, source_target_pairs={{8,1},{9,2},{10,3},{11,4},{12,5},{13,6},{14,7},{16,9},{17,10},{18,... | collective-permute-start | bytes 24584 | tf_op jit(solution)/shard_map/ppermute | solution.py:186
  61.9 12.0 %collective-permute-start = (f32[25,8,256]{2,1,0:T(8,128)S(1)}, f32[25,8,256]{2,1,0:T(8,128)S(1)}, u32[]{:S(2)}, u32[]{:S(2)}) collective-permute-start(f32[25,8,256]{2,1,0:T(8,128)S(1)} %get-tuple-element.18), channel_id=1, source_target_pairs={{0,8},{1,9},{2,10},{3,11},{4,12},{5,13},{6,14},{7,15},{8,16},{9,17... | collective-permute-start | bytes 614408 | tf_op jit(solution)/shard_map/ppermute | solution.py:186
  68.7 12.9 %collective-permute-start.1 = (f32[25,8,256]{2,1,0:T(8,128)S(1)}, f32[25,8,256]{2,1,0:T(8,128)S(1)}, u32[]{:S(2)}, u32[]{:S(2)}) collective-permute-start(f32[25,8,256]{2,1,0:T(8,128)S(1)} %get-tuple-element.19), channel_id=1, source_target_pairs={{8,0},{9,1},{10,2},{11,3},{12,4},{13,5},{14,6},{15,7},{16,8},{17,9... | collective-permute-start | bytes 614408 | tf_op jit(solution)/shard_map/ppermute | solution.py:186
  110.1 18.8 %all-to-all-start.1 = ((f32[32,16,256]{2,1,0:T(8,128)}), f32[32,16,256]{2,1,0:T(8,128)S(1)}, u32[]{:S(2)}, u32[]{:S(2)}) async-start(f32[32,16,256]{2,1,0:T(8,128)} %answer.1), calls=%async_computation.1 | async-start | bytes 1048576 | tf_op jit(solution)/shard_map/all_to_all | solution.py:365
  129.0 0.8 copy-start

commit v2 on v1

--- a/solution.py
+++ b/solution.py
@@ -174,28 +174,116 @@
     )(recv, prev, scale)
 
 
+MESH = pl.DeviceIdType.MESH
+ANY = pl.BlockSpec(memory_space=pl.ANY)
+AROUND = [(1, 0), (-1, 0), (0, 1), (0, -1), (1, 1), (1, -1), (-1, 1), (-1, -1)]
+
+
+def exchange_kernel(groups, members, rows, edge, strip, edges, strips, corners, send, recv):
+    g, d = lax.axis_index("grp"), lax.axis_index("dev")
+
+    def exists(up, right):
+        row, col = g + up, d + right
+        return (row >= 0) & (row < groups) & (col >= 0) & (col < members)
+
+    barrier = pltpu.get_barrier_semaphore()
+    for up, right in AROUND:
+
+        @pl.when(exists(up, right))
+        def _():
+            pl.semaphore_signal(barrier, inc=1, device_id=(g + up, d + right), device_id_type=MESH)
+
+    one = lambda condition: jnp.where(condition, 1, 0).astype(jnp.int32)
+    near_rows = 1 + one(g > 0) + one(g < groups - 1)
+    near_cols = 1 + one(d > 0) + one(d < members - 1)
+    pl.semaphore_wait(barrier, near_rows * near_cols - 1)
+
+    copies = []
+    for k, (up, right) in enumerate(AROUND):
+        v, h = (0 if up == 1 else 1), (0 if right == 1 else 1)
+        if right == 0:
+            source, target = edge.at[1 - v], edges.at[v]
+        elif up == 0:
+            source, target = strip.at[1 - h], strips.at[h]
+        else:
+            start = rows - SWEEPS if up == 1 else 0
+            source, target = strip.at[1 - h, :, pl.ds(start, SWEEPS), :], corners.at[v, h]
+        copy = pltpu.make_async_remote_copy(
+            src_ref=source, dst_ref=target, send_sem=send.at[k], recv_sem=recv.at[k],
+            device_id=(g + up, d + right), device_id_type=MESH,
+        )
+        copies.append(copy)
+        pl.when(exists(up, right))(copy.start)
+    for k, (up, right) in enumerate(AROUND):
+        pl.when(exists(up, right))(copies[k].wait_send)
+        pl.when(exists(-up, -right))(copies[k].wait_recv)
+
+
 def exchange(edge, strip, rows):
     groups, members = lax.axis_size("grp"), lax.axis_size("dev")
-
-    def move(x, up, right):
-        pairs = []
-        for g in range(groups):
-            for d in range(members):
-                if 0 <= g + up < groups and 0 <= d + right < members:
-                    pairs.append((g * members + d, (g + up) * members + d + right))
-        return lax.ppermute(x, ("grp", "dev"), pairs)
-
-    edges = jnp.stack([move(edge[1], 1, 0), move(edge[0], -1, 0)])
-    strips = jnp.stack([move(strip[1], 0, 1), move(strip[0], 0, -1)])
-    corners = jnp.stack([
-        jnp.stack([move(strip[1][:, rows - SWEEPS :], 1, 1), move(strip[0][:, rows - SWEEPS :], 1, -1)]),
-        jnp.stack([move(strip[1][:, :SWEEPS], -1, 1), move(strip[0][:, :SWEEPS], -1, -1)]),
-    ])
-    return edges, strips, corners
+    shapes = [edge.shape, strip.shape, (2, 2, 2, SWEEPS, LANES)]
+    return pl.pallas_call(
+        functools.partial(exchange_kernel, groups, members, rows),
+        in_specs=[ANY, ANY],
+        out_specs=[ANY] * 3,
+        out_shape=[jax.ShapeDtypeStruct(s, F32) for s in shapes],
+        scratch_shapes=[pltpu.SemaphoreType.DMA((8,)), pltpu.SemaphoreType.DMA((8,))],
+        compiler_params=pltpu.CompilerParams(collective_id=0, has_side_effects=True),
+        name="exchange",
+    )(edge, strip)
+
+
+def swap_kernel(n, members, x, y, send, recv, own):
+    me = lax.axis_index("grp") * members + lax.axis_index("dev")
+    place = lambda k: lax.rem(me + k, n)
+    ident = lambda t: (t // members, lax.rem(t, members))
+    barrier = pltpu.get_barrier_semaphore()
+
+    def greet(k, carry):
+        pl.semaphore_signal(barrier, inc=1, device_id=ident(place(k)), device_id_type=MESH)
+        return carry
+
+    lax.fori_loop(1, n, greet, 0)
+    keep = pltpu.make_async_copy(x.at[me], y.at[me], own)
+    keep.start()
+    pl.semaphore_wait(barrier, n - 1)
+
+    def copy(k):
+        target = place(k)
+        return pltpu.make_async_remote_copy(
+            src_ref=x.at[target], dst_ref=y.at[me], send_sem=send.at[k], recv_sem=recv.at[k],
+            device_id=ident(target), device_id_type=MESH,
+        )
+
+    def begin(k, carry):
+        copy(k).start()
+        return carry
+
+    def end(k, carry):
+        copy(k).wait()
+        return carry
+
+    lax.fori_loop(1, n, begin, 0)
+    keep.wait()
+    lax.fori_loop(1, n, end, 0)
+
+
+def swap(x, number):
+    n = x.shape[0]
+    return pl.pallas_call(
+        functools.partial(swap_kernel, n, lax.axis_size("dev")),
+        in_specs=[ANY],
+        out_specs=ANY,
+        out_shape=jax.ShapeDtypeStruct(x.shape, F32),
+        scratch_shapes=[pltpu.SemaphoreType.DMA((n,)), pltpu.SemaphoreType.DMA((n,)),
+                        pltpu.SemaphoreType.DMA],
+        compiler_params=pltpu.CompilerParams(collective_id=number, has_side_effects=True),
+        name=("swap_out", "swap_back")[number - 1],
+    )(x)
 
 
 def sweep_kernel(rows, cols, prev_ref, load_ref, scale_ref, edge_ref, strip_ref, corner_ref,
-                 inverse_ref, out_ref, one, two, base, factor):
+                 inverse_ref, flag_ref, out_ref, one, two, base, factor):
     top = 2 * SWEEPS
     wide = cols + LANES
     tall = rows + 2 * top
@@ -206,13 +294,17 @@
     one[:, top : top + rows, :cols] = prev_ref[...]
     base[:, top : top + rows, :cols] = load_ref[...]
     factor[top : top + rows, :cols] = scale_ref[...]
+    near = [flag_ref[k] > 0 for k in range(4)]
     for side, start in ((0, top - SWEEPS), (1, top + rows)):
-        one[:, start : start + SWEEPS, :cols] = edge_ref[side, :12]
-        base[:, start : start + SWEEPS, :cols] = edge_ref[side, 13:]
-        factor[start : start + SWEEPS, :cols] = edge_ref[side, 12]
-
-    def unpack(west, east, start, kind):
+        shell = jnp.where(near[side], edge_ref[side], 0.0)
+        one[:, start : start + SWEEPS, :cols] = shell[:12]
+        base[:, start : start + SWEEPS, :cols] = shell[13:]
+        factor[start : start + SWEEPS, :cols] = shell[12]
+
+    def unpack(west, east, start, kind, at_all):
         size = west.shape[0]
+        west = jnp.where(near[2] & at_all, west, 0.0)
+        east = jnp.where(near[3] & at_all, east, 0.0)
         lane = lax.broadcasted_iota(jnp.int32, (size, LANES), 1)
         for j in range(13 if kind == 0 else 12):
             back = (LANES - j * SWEEPS) % LANES
@@ -228,9 +320,9 @@
                 base[j, start : start + size, cols:] = piece
 
     for kind in range(2):
-        unpack(strip_ref[0, kind], strip_ref[1, kind], top, kind)
+        unpack(strip_ref[0, kind], strip_ref[1, kind], top, kind, near[2] | near[3])
         for side, start in ((0, top - SWEEPS), (1, top + rows)):
-            unpack(corner_ref[side, 0, kind], corner_ref[side, 1, kind], start, kind)
+            unpack(corner_ref[side, 0, kind], corner_ref[side, 1, kind], start, kind, near[side])
 
     starts = list(range(top - SWEEPS, top + rows + SWEEPS, 8))
     for start in starts:
@@ -246,7 +338,7 @@
             base[i, here, :] = total * inv
         factor[here, :] = inv * coupling_weight
 
-    def relax(source, target, wanted):
+    def relax(source, target, wanted, offset=0):
         for start in wanted:
             here = slice(start, start + 8)
             south = slice(start - 1, start + 7)
@@ -265,27 +357,33 @@
                 total = inverse_ref[i, 0] * sources[0]
                 for j in range(1, 12):
                     total = total + inverse_ref[i, j] * sources[j]
-                target[i, here, :] = base[i, here, :] + total * inv
+                total = base[i, here, :] + total * inv
+                target[i, start - offset : start - offset + 8, :] = total[:, : target.shape[2]]
 
     def pair(_, carry):
         relax(one, two, starts)
         relax(two, one, starts)
         return carry
 
-    lax.fori_loop(0, SWEEPS // 2, pair, 0)
-    out_ref[...] = one[:, top : top + rows, :cols]
+    lax.fori_loop(0, SWEEPS // 2 - 1, pair, 0)
+    relax(one, two, starts)
+    relax(two, out_ref, starts[1:-1], top)
 
 
 def sweep(rows, cols, prev, load, scale, edges, strips, corners, inverse):
     tall, wide = rows + 4 * SWEEPS, cols + LANES
+    g, d = lax.axis_index("grp"), lax.axis_index("dev")
+    flags = jnp.stack(
+        [g > 0, g < lax.axis_size("grp") - 1, d > 0, d < lax.axis_size("dev") - 1]
+    ).astype(jnp.int32)
     return pl.pallas_call(
         functools.partial(sweep_kernel, rows, cols),
-        in_specs=[VM] * 6 + [SM],
+        in_specs=[VM] * 6 + [SM] * 2,
         out_specs=VM,
         out_shape=jax.ShapeDtypeStruct((12, rows, cols), F32),
         scratch_shapes=[pltpu.VMEM((12, tall, wide), F32)] * 3 + [pltpu.VMEM((tall, wide), F32)],
         name="sweep",
-    )(prev, load, scale, edges, strips, corners, inverse)
+    )(prev, load, scale, edges, strips, corners, inverse, flags)
 
 
 def answer_kernel(rows, cols, disp_ref, recv_ref, out_ref, table):
@@ -341,8 +439,9 @@
     node = jnp.zeros((16, width), F32)
     for d in range(n):
         node = jnp.where(owner == d, picked[d * 16 : (d + 1) * 16], node)
-    for c in range(3):
-        out_ref[c] = jnp.dot(spread_ref[c], node, precision=highest, preferred_element_type=F32)
+    faced = jnp.dot(spread_ref[...], node, precision=highest, preferred_element_type=F32)
+    for k in range(NODES_F):
+        out_ref[k] = faced[8 * k : 8 * k + 3]
 
 
 def finish(n, cap, back, owner, rank, spread):
@@ -353,16 +452,12 @@
         functools.partial(finish_kernel, n, cap),
         grid=(faces // width,),
         in_specs=[pl.BlockSpec((n * 16, cap), lambda i: (0, 0)), row, row,
-                  pl.BlockSpec(spread.shape, lambda i: (0, 0, 0))],
-        out_specs=pl.BlockSpec((3, NODES_F, width), lambda i: (0, 0, i)),
-        out_shape=jax.ShapeDtypeStruct((3, NODES_F, faces), F32),
+                  pl.BlockSpec(spread.shape, lambda i: (0, 0))],
+        out_specs=pl.BlockSpec((NODES_F, 3, width), lambda i: (0, 0, i)),
+        out_shape=jax.ShapeDtypeStruct((NODES_F, 3, faces), F32),
         scratch_shapes=[pltpu.VMEM((n * 16, 2 * cap), BF16)],
         name="finish",
     )(back, owner, rank, spread)
-
-
-def swap(x):
-    return lax.all_to_all(x, ("grp", "dev"), split_axis=0, concat_axis=0, tiled=True)
 
 
 def local(
@@ -384,12 +479,14 @@
     owner = face_owner.reshape(1, faces)
     spread = jnp.einsum("nk,cd->ncdk", transfer, jnp.eye(3, dtype=F32), precision=highest)
     spread_in = jnp.pad(spread.reshape(12, 3 * NODES_F), ((0, 4), (0, 0)))
-    spread_out = jnp.pad(spread.transpose(2, 3, 0, 1).reshape(3, NODES_F, 12), ((0, 0), (0, 0), (0, 4)))
+    spread_out = jnp.pad(
+        spread.transpose(3, 2, 0, 1).reshape(NODES_F, 3, 12), ((0, 0), (0, 5), (0, 4))
+    ).reshape(8 * NODES_F, 16)
     outgoing, rank, inverse = route(
         n, cap, cols, owner, face_element.reshape(1, faces), element_state, lift,
         face_scale.reshape(1, faces), spread_in, stiffness_ref,
     )
-    received = swap(outgoing.reshape(n, 16, cap))
+    received = swap(outgoing.reshape(n, 16, cap), 1)
     fold = max(1, LANES // cap)
     if fold > 1:
         received = received.reshape(n // fold, fold, 16, cap).transpose(0, 2, 1, 3)
@@ -401,9 +498,9 @@
     if fold > 1:
         returning = returning.reshape(n // fold, 16, fold, cap).transpose(0, 2, 1, 3)
         returning = returning.reshape(n, 16, cap)
-    back = swap(returning).reshape(n * 16, cap)
+    back = swap(returning, 2).reshape(n * 16, cap)
     face_displacement = finish(n, cap, back, owner, rank, spread_out)
-    return (disp.reshape(4, 3, rows, cols), face_displacement)
+    return (disp.reshape(4, 3, rows, cols), face_displacement.transpose(1, 0, 2))
 
 
 def solution(mesh):

time: 140 us -> 112 us (0.80)
  Pallas kernels: 57.4 us -> 108 us
  waiting for transfers between devices: 25.8 us -> 0 us
  blocking collectives: 23.7 us -> 0 us
  starting transfers between devices: 22.4 us -> 0 us
  local copies, waits for them, and re-layouts: 7.14 us -> 2.09 us
  other arithmetic: 2.16 us -> 0.7 us
    pallas_call x0 -> x3, Pallas kernels: none -> 51.1 us  [the longest x2 37.4 us: swap(): pl.pallas_call(functools.partial(swap_kernel, n, lax.axis_size('dev')), i...]
    all_to_all x1 -> x0, blocking collectives: 23.7 us -> none  [swap(): lax.all_to_all(x, ('grp', 'dev'), split_axis=0, concat_axis=0, tiled=True)]
    ppermute x8 -> x0, starting transfers between devices: 19.8 us -> none  [move(): return lax.ppermute(x, ('grp', 'dev'), pairs)]
    all_to_all x1 -> x0, waiting for transfers between devices: 15.5 us -> none  [swap(): lax.all_to_all(x, ('grp', 'dev'), split_axis=0, concat_axis=0, tiled=True)]
    ppermute x8 -> x0, waiting for transfers between devices: 10.3 us -> none  [move(): return lax.ppermute(x, ('grp', 'dev'), pairs)]
    unnamed x5 -> x3, local copies, waits for them, and re-layouts: 3.76 us -> 0.77 us
    all_to_all x1 -> x0, starting transfers between devices: 2.61 us -> none  [swap(): lax.all_to_all(x, ('grp', 'dev'), split_axis=0, concat_axis=0, tiled=True)]
    another operation x6 -> x1, other arithmetic: 2.09 us -> 0.01 us  [the longest x1 0.79 us: exchange(): edges = jnp.stack([move(edge[1], 1, 0), move(edge[0], -1, 0)])]
  transfers between devices with their start and end apart: 9 -> 0, of which waited for: 3 -> 0; matrix products, arithmetic and copies ran while one was open for 2% -> 0% of each run, Pallas kernels for 0% -> 0%
where the time goes in v2:
time: 112 us
  Pallas kernels  108 us (96%)
  local copies, waits for them, and re-layouts  2.09 us (2%)
    pallas_call x2, Pallas kernels, swap(): pl.pallas_call(functools.partial(swap_kernel, n, lax.axis_size('dev')), i...  37.4 us
    pallas_call x1, Pallas kernels, sweep(): pl.pallas_call(functools.partial(sweep_kernel, rows, cols), in_specs=[VM]...  16.8 us
    pallas_call x1, Pallas kernels, exchange(): pl.pallas_call(functools.partial(exchange_kernel, groups, members, rows),...  13.7 us
    pallas_call x1, Pallas kernels, route(): pl.pallas_call(functools.partial(route_kernel, n, cap, cols), grid=(faces...  11.3 us
    pallas_call x1, Pallas kernels, collect(): pl.pallas_call(functools.partial(gather_kernel_in, rows, cols), grid=(gro...  11.1 us
    pallas_call x1, Pallas kernels, answer(): pl.pallas_call(functools.partial(answer_kernel, rows, cols), grid=(groups...  10.1 us
    pallas_call x1, Pallas kernels, finish(): pl.pallas_call(functools.partial(finish_kernel, n, cap), grid=(faces // w...  7.64 us

profile of v2, /device:TPU:0, one launch (start us, length us, event | category | flops | bytes accessed | tf_op | source)
XLA Modules:
  0.0 111.5 jit_solution(6523132851299143825)
XLA Ops:
  0.6 0.0 copy-start
  0.7 0.7 copy-done
  1.3 0.1 broadcast_multiply_fusion
  1.4 0.1 reshape.38
  1.5 0.6 pad.8.spread_ref
  2.1 11.3 %route.1 = (f32[512,256]{1,0:T(8,128)}, f32[1,4096]{1,0:T(1,128)}, f32[12,12]{1,0:T(8,128)}) custom-call(s32[1,4096]{1,0:T(1,128)} %bitcast.26, s32[1,4096]{1,0:T(1,128)} %bitcast.28, bf16[110,4096]{1,0:T(8,128)(2,1)} %state_ref.1, bf16[30,110]{1,0:T(8,128)(2,1)} %lift_ref.1, f32[1,4096]{1,0:T(1,128)} %bitcast.29, f32[16,30]{1,0:T(8,128)} %pad.8.spread_ref, ...), custom_call_target="tpu_custom_call" | custom-call | tf_op jit(solution)/shard_map/route/pallas_call | solution.py:96
  13.4 19.9 %swap_out.1.recv_ref = f32[32,16,256]{2,1,0:T(8,128)} custom-call(f32[32,16,256]{2,1,0:T(8,128)} %bitcast.24), custom_call_target="tpu_custom_call" | custom-call | tf_op jit(solution)/shard_map/swap_out/pallas_call | solution.py:273
  33.2 11.1 %collect.1 = (f32[12,64,256]{2,1,0:T(8,128)}, f32[2,25,8,256]{3,2,1,0:T(8,128)}, f32[2,2,64,128]{3,2,1,0:T(8,128)}) custom-call(f32[32,16,256]{2,1,0:T(8,128)} %swap_out.1.recv_ref, f32[12,64,256]{2,1,0:T(8,128)} %bitcast.20, f32[64,256]{1,0:T(8,128)} %scale_ref.3), custom_call_target="tpu_custom_call" | custom-call | tf_op jit(solution)/shard_map/collect/pallas_call | solution.py:166
  44.3 13.7 %exchange.1 = (f32[2,25,8,256]{3,2,1,0:T(8,128)}, f32[2,2,64,128]{3,2,1,0:T(8,128)}, f32[2,2,2,8,128]{4,3,2,1,0:T(8,128)}) custom-call(f32[2,25,8,256]{3,2,1,0:T(8,128)} %get-tuple-element.13.edge, f32[2,2,64,128]{3,2,1,0:T(8,128)} %get-tuple-element.14.strip), custom_call_target="tpu_custom_call" | custom-call | tf_op jit(solution)/shard_map/exchange/pallas_call | solution.py:225
  58.0 0.6 add_convert_fusion.flag_ref
  58.7 16.8 %sweep.1.disp_ref = f32[12,64,256]{2,1,0:T(8,128)} custom-call(f32[12,64,256]{2,1,0:T(8,128)} %bitcast.21, f32[12,64,256]{2,1,0:T(8,128)} %get-tuple-element.12.load_ref, f32[64,256]{1,0:T(8,128)} %scale_ref.3, f32[2,25,8,256]{3,2,1,0:T(8,128)} %get-tuple-element.15.edge_ref, f32[2,2,64,128]{3,2,1,0:T(8,128)} %get-tuple-element.16.strip_ref, ...), custom_call_target="tpu_custom_call" | custom-call | tf_op jit(solution)/shard_map/sweep/pallas_call | solution.py:379
  75.5 10.1 %answer.1.x = f32[32,16,256]{2,1,0:T(8,128)} custom-call(f32[12,64,256]{2,1,0:T(8,128)} %sweep.1.disp_ref, f32[32,16,256]{2,1,0:T(8,128)} %swap_out.1.recv_ref), custom_call_target="tpu_custom_call" | custom-call | tf_op jit(solution)/shard_map/answer/pallas_call | solution.py:416
  85.6 17.5 %swap_back.1 = f32[32,16,256]{2,1,0:T(8,128)} custom-call(f32[32,16,256]{2,1,0:T(8,128)} %answer.1.x), custom_call_target="tpu_custom_call" | custom-call | tf_op jit(solution)/shard_map/swap_back/pallas_call | solution.py:273
  103.1 0.1 copy.13
  103.2 0.6 pad_bitcast_fusion.spread_ref
  103.9 7.6 %finish.1 = f32[10,3,4096]{2,1,0:T(4,128)} custom-call(f32[512,256]{1,0:T(8,128)} %bitcast.22, s32[1,4096]{1,0:T(1,128)} %bitcast.27, f32[1,4096]{1,0:T(1,128)} %get-tuple-element.19.rank_ref, f32[80,16]{1,0:T(8,128)} %pad_bitcast_fusion.spread_ref), custom_call_target="tpu_custom_call" | custom-call | tf_op jit(solution)/shard_map/finish/pallas_call | solution.py:451
  (1 shorter events, 0.0 us)
Async XLA Ops:
  0.6 0.7 copy-start

commit v3 on v2

--- a/solution.py
+++ b/solution.py
@@ -386,6 +386,11 @@
     )(prev, load, scale, edges, strips, corners, inverse, flags)
 
 
+def shape_back(cap):
+    halves = max(1, cap // LANES)
+    return halves, -(-12 * halves // 8) * 8
+
+
 def answer_kernel(rows, cols, disp_ref, recv_ref, out_ref, table):
     @pl.when(pl.program_id(0) == 0)
     def _():
@@ -404,21 +409,28 @@
         jnp.sum(jnp.where(mask, picked[c * rows : (c + 1) * rows], 0.0), axis=0, keepdims=True)
         for c in range(12)
     ]
-    result = jnp.concatenate(lines + [jnp.zeros((4, width), F32)], axis=0)
+    halves, deep = shape_back(cap)
+    lanes = cap // halves
+    result = jnp.concatenate(lines, axis=0)
+    pad = [jnp.zeros((deep - 12 * halves, lanes), F32)] if deep > 12 * halves else []
     for g in range(recv_ref.shape[0]):
-        out_ref[g] = result[:, g * cap : (g + 1) * cap]
+        parts = [
+            result[:, g * cap + h * lanes : g * cap + (h + 1) * lanes] for h in range(halves)
+        ]
+        out_ref[g] = jnp.concatenate(parts + pad, axis=0)
 
 
 def answer(rows, cols, disp, recv):
     groups, _, cap = recv.shape
     block = max(1, min(groups, 1024 // cap))
+    halves, deep = shape_back(cap)
     spec = pl.BlockSpec((block, 16, cap), lambda i: (i, 0, 0))
     return pl.pallas_call(
         functools.partial(answer_kernel, rows, cols),
         grid=(groups // block,),
         in_specs=[pl.BlockSpec(disp.shape, lambda i: (0, 0, 0)), spec],
-        out_specs=spec,
-        out_shape=jax.ShapeDtypeStruct(recv.shape, F32),
+        out_specs=pl.BlockSpec((block, deep, cap // halves), lambda i: (i, 0, 0)),
+        out_shape=jax.ShapeDtypeStruct((groups, deep, cap // halves), F32),
         scratch_shapes=[pltpu.VMEM((12 * rows, 2 * cols), BF16)],
         name="answer",
     )(disp, recv)
@@ -430,15 +442,22 @@
         high, low = split(back_ref[...])
         table[...] = jnp.concatenate([high.astype(BF16), low.astype(BF16)], axis=1)
 
-    slot_hot = one_hot(rank_ref[...], cap)
+    halves, deep = shape_back(cap)
+    lanes = cap // halves
+    rank = rank_ref[...].astype(jnp.int32)
+    part = rank // lanes
+    slot_hot = one_hot((rank - part * lanes).astype(F32), lanes)
     picked = jnp.dot(
         table[...], jnp.concatenate([slot_hot, slot_hot], axis=0), preferred_element_type=F32
     )
     width = owner_ref.shape[1]
-    owner = jnp.broadcast_to(owner_ref[...], (16, width))
-    node = jnp.zeros((16, width), F32)
+    owner = jnp.broadcast_to(owner_ref[...], (deep, width))
+    found = jnp.zeros((deep, width), F32)
     for d in range(n):
-        node = jnp.where(owner == d, picked[d * 16 : (d + 1) * 16], node)
+        found = jnp.where(owner == d, picked[d * deep : (d + 1) * deep], found)
+    node = found[:12]
+    for h in range(1, halves):
+        node = jnp.where(part == h, found[12 * h : 12 * h + 12], node)
     faced = jnp.dot(spread_ref[...], node, precision=highest, preferred_element_type=F32)
     for k in range(NODES_F):
         out_ref[k] = faced[8 * k : 8 * k + 3]
@@ -451,11 +470,11 @@
     return pl.pallas_call(
         functools.partial(finish_kernel, n, cap),
         grid=(faces // width,),
-        in_specs=[pl.BlockSpec((n * 16, cap), lambda i: (0, 0)), row, row,
+        in_specs=[pl.BlockSpec(back.shape, lambda i: (0, 0)), row, row,
                   pl.BlockSpec(spread.shape, lambda i: (0, 0))],
         out_specs=pl.BlockSpec((NODES_F, 3, width), lambda i: (0, 0, i)),
         out_shape=jax.ShapeDtypeStruct((NODES_F, 3, faces), F32),
-        scratch_shapes=[pltpu.VMEM((n * 16, 2 * cap), BF16)],
+        scratch_shapes=[pltpu.VMEM((back.shape[0], 2 * back.shape[1]), BF16)],
         name="finish",
     )(back, owner, rank, spread)
 
@@ -480,8 +499,8 @@
     spread = jnp.einsum("nk,cd->ncdk", transfer, jnp.eye(3, dtype=F32), precision=highest)
     spread_in = jnp.pad(spread.reshape(12, 3 * NODES_F), ((0, 4), (0, 0)))
     spread_out = jnp.pad(
-        spread.transpose(3, 2, 0, 1).reshape(NODES_F, 3, 12), ((0, 0), (0, 5), (0, 4))
-    ).reshape(8 * NODES_F, 16)
+        spread.transpose(3, 2, 0, 1).reshape(NODES_F, 3, 12), ((0, 0), (0, 5), (0, 0))
+    ).reshape(8 * NODES_F, 12)
     outgoing, rank, inverse = route(
         n, cap, cols, owner, face_element.reshape(1, faces), element_state, lift,
         face_scale.reshape(1, faces), spread_in, stiffness_ref,
@@ -498,7 +517,8 @@
     if fold > 1:
         returning = returning.reshape(n // fold, 16, fold, cap).transpose(0, 2, 1, 3)
         returning = returning.reshape(n, 16, cap)
-    back = swap(returning, 2).reshape(n * 16, cap)
+    back = swap(returning, 2)
+    back = back.reshape(-1, back.shape[2])
     face_displacement = finish(n, cap, back, owner, rank, spread_out)
     return (disp.reshape(4, 3, rows, cols), face_displacement.transpose(1, 0, 2))
 

time: 112 us -> 109 us (0.973)
  Pallas kernels: 108 us -> 105 us
    pallas_call x2, Pallas kernels: 37.4 us -> 34.7 us  [swap(): pl.pallas_call(functools.partial(swap_kernel, n, lax.axis_size('dev')), i...]
where the time goes in v3:
time: 109 us; the launch traced here: 108 us
  Pallas kernels  105 us (96%)
  local copies, waits for them, and re-layouts  2.08 us (2%)
    pallas_call x2, Pallas kernels, swap(): pl.pallas_call(functools.partial(swap_kernel, n, lax.axis_size('dev')), i...  34.7 us
    pallas_call x1, Pallas kernels, sweep(): pl.pallas_call(functools.partial(sweep_kernel, rows, cols), in_specs=[VM]...  16.8 us
    pallas_call x1, Pallas kernels, exchange(): pl.pallas_call(functools.partial(exchange_kernel, groups, members, rows),...  13.7 us
    pallas_call x1, Pallas kernels, route(): pl.pallas_call(functools.partial(route_kernel, n, cap, cols), grid=(faces...  11.3 us
    pallas_call x1, Pallas kernels, collect(): pl.pallas_call(functools.partial(gather_kernel_in, rows, cols), grid=(gro...  11.1 us
    pallas_call x1, Pallas kernels, answer(): pl.pallas_call(functools.partial(answer_kernel, rows, cols), grid=(groups...  10.1 us
    pallas_call x1, Pallas kernels, finish(): pl.pallas_call(functools.partial(finish_kernel, n, cap), grid=(faces // w...  7.16 us

profile of v3, /device:TPU:0, one launch (start us, length us, event | category | flops | bytes accessed | tf_op | source)
XLA Modules:
  0.0 108.3 jit_solution(955232947367796604)
XLA Ops:
  0.6 0.0 copy-start
  0.7 0.7 copy-done
  1.3 0.1 broadcast_multiply_fusion
  1.4 0.1 reshape.38
  1.5 0.6 pad.8.spread_ref
  2.1 11.3 %route.1 = (f32[512,256]{1,0:T(8,128)}, f32[1,4096]{1,0:T(1,128)}, f32[12,12]{1,0:T(8,128)}) custom-call(s32[1,4096]{1,0:T(1,128)} %bitcast.26, s32[1,4096]{1,0:T(1,128)} %bitcast.28, bf16[110,4096]{1,0:T(8,128)(2,1)} %state_ref.1, bf16[30,110]{1,0:T(8,128)(2,1)} %lift_ref.1, f32[1,4096]{1,0:T(1,128)} %bitcast.29, f32[16,30]{1,0:T(8,128)} %pad.8.spread_ref, ...), custom_call_target="tpu_custom_call" | custom-call | tf_op jit(solution)/shard_map/route/pallas_call | solution.py:96
  13.4 19.9 %swap_out.1.recv_ref = f32[32,16,256]{2,1,0:T(8,128)} custom-call(f32[32,16,256]{2,1,0:T(8,128)} %bitcast.24), custom_call_target="tpu_custom_call" | custom-call | tf_op jit(solution)/shard_map/swap_out/pallas_call | solution.py:273
  33.2 11.1 %collect.1 = (f32[12,64,256]{2,1,0:T(8,128)}, f32[2,25,8,256]{3,2,1,0:T(8,128)}, f32[2,2,64,128]{3,2,1,0:T(8,128)}) custom-call(f32[32,16,256]{2,1,0:T(8,128)} %swap_out.1.recv_ref, f32[12,64,256]{2,1,0:T(8,128)} %bitcast.19, f32[64,256]{1,0:T(8,128)} %scale_ref.3), custom_call_target="tpu_custom_call" | custom-call | tf_op jit(solution)/shard_map/collect/pallas_call | solution.py:166
  44.3 13.7 %exchange.1 = (f32[2,25,8,256]{3,2,1,0:T(8,128)}, f32[2,2,64,128]{3,2,1,0:T(8,128)}, f32[2,2,2,8,128]{4,3,2,1,0:T(8,128)}) custom-call(f32[2,25,8,256]{3,2,1,0:T(8,128)} %get-tuple-element.13.edge, f32[2,2,64,128]{3,2,1,0:T(8,128)} %get-tuple-element.14.strip), custom_call_target="tpu_custom_call" | custom-call | tf_op jit(solution)/shard_map/exchange/pallas_call | solution.py:225
  58.0 0.6 add_convert_fusion.flag_ref
  58.7 16.8 %sweep.1.disp_ref = f32[12,64,256]{2,1,0:T(8,128)} custom-call(f32[12,64,256]{2,1,0:T(8,128)} %bitcast.20, f32[12,64,256]{2,1,0:T(8,128)} %get-tuple-element.12.load_ref, f32[64,256]{1,0:T(8,128)} %scale_ref.3, f32[2,25,8,256]{3,2,1,0:T(8,128)} %get-tuple-element.15.edge_ref, f32[2,2,64,128]{3,2,1,0:T(8,128)} %get-tuple-element.16.strip_ref, ...), custom_call_target="tpu_custom_call" | custom-call | tf_op jit(solution)/shard_map/sweep/pallas_call | solution.py:379
  75.5 10.1 %answer.1.x = f32[32,24,128]{2,1,0:T(8,128)} custom-call(f32[12,64,256]{2,1,0:T(8,128)} %sweep.1.disp_ref, f32[32,16,256]{2,1,0:T(8,128)} %swap_out.1.recv_ref), custom_call_target="tpu_custom_call" | custom-call | tf_op jit(solution)/shard_map/answer/pallas_call | solution.py:428
  85.6 14.8 %swap_back.1 = f32[32,24,128]{2,1,0:T(8,128)} custom-call(f32[32,24,128]{2,1,0:T(8,128)} %answer.1.x), custom_call_target="tpu_custom_call" | custom-call | tf_op jit(solution)/shard_map/swap_back/pallas_call | solution.py:273
  100.5 0.1 copy.13
  100.6 0.6 pad_bitcast_fusion.spread_ref
  101.2 7.2 %finish.1 = f32[10,3,4096]{2,1,0:T(4,128)} custom-call(f32[768,128]{1,0:T(8,128)} %bitcast.22, s32[1,4096]{1,0:T(1,128)} %bitcast.27, f32[1,4096]{1,0:T(1,128)} %get-tuple-element.19.rank_ref, f32[80,12]{1,0:T(8,128)} %pad_bitcast_fusion.spread_ref), custom_call_target="tpu_custom_call" | custom-call | tf_op jit(solution)/shard_map/finish/pallas_call | solution.py:470
  (1 shorter events, 0.0 us)
Async XLA Ops:
  0.6 0.7 copy-start
